TPU v7x, 32 devices: a whole 2x2x4 slice. The times are simulated.
32 devices in a mesh: row: 16 (over z, x, core), col: 2 (over y).
Axes of the slice: x: 2, y: 2, z: 4, core: 2. Of those that a mesh axis runs over, the one named last changes fastest.
Arguments:
- tiles: bfloat16 [16, 2, 256, 128, 128], P('row', 'col'), may hold values from 0 to 0.00064849854
- tile_row: int32 [16, 2, 256], P('row', 'col'), may hold values from 0 to 16, as said below
- tile_col: int32 [16, 2, 256], P('row', 'col'), may hold values from 0 to 128, as said below
- right_vecs: bfloat16 [256, 32, 128], P(('row', 'col')), may hold values from -6 to 6
- left_vecs: bfloat16 [256, 32, 128], P(('row', 'col')), may hold values from -6 to 6
Outputs:
- right_next: float32 [256, 32, 128], P(('row', 'col'))
- left_next: float32 [256, 32, 128], P(('row', 'col'))
- gram: float32 [32, 32], replicated
Inputs may be any that keep to these rules, and one draw needn't show every extreme that they name: Value 16 marks an empty slot; a slot is empty in tile_row exactly when it is empty in tile_col; live slots come first on each device; each device has 128 to 256 live slots and some device has all 256 live. `tile_col`: value 128 marks an empty slot, in the same slots as tile_row.
All inputs are finite; a program needn't handle non-finite values.
Results may differ from a plain program's by a relative error of at most 0.0003.
Values may be sent and summed in bfloat16 or wider, within the bound.
A program may use at most 64 MiB of HBM per device.

v0:
```python
import functools

import jax
import jax.numpy as jnp
from jax import lax
from jax.experimental import pallas as pl
from jax.experimental.pallas import tpu as pltpu
from jax.sharding import PartitionSpec as P

MESH = pl.DeviceIdType.MESH
F32 = jnp.float32
BF16 = jnp.bfloat16
GROUP = 32
PAIR = 2
KGROUP = 8
TOP = 32767.0
LEAST = 2.0**-110
PAD = 1


def split(value):
    high = value.astype(BF16)
    low = (value - high.astype(F32)).astype(BF16)
    return high, low


def mul(a, b, dims=(((1,), (0,)), ((), ()))):
    return lax.dot_general(a, b, dims, preferred_element_type=F32)


def kernel(
    sizes,
    row_s,
    col_s,
    row_v,
    col_v,
    right,
    left,
    tiles,
    out_y,
    out_z,
    out_g,
    tbuf,
    cv,
    rv,
    prod,
    zp,
    zc,
    zs,
    qx_out,
    sx_out,
    qx,
    sx,
    qz_out,
    sz_out,
    qz,
    sz,
    yp,
    yl,
    ga,
    gb,
    tile_sem,
    send_sem,
    left_sem,
    right_sem,
    zc_sem,
    zx_sem,
    zz_sem,
    sx_sem,
    sz_sem,
    y_sem,
    g_sem,
):
    n_r, n_c, outer, inner, chunks = sizes
    piece, vecs, side = right.shape
    slots = tbuf.shape[0]
    step = slots // chunks
    block_rows = piece * n_c
    block_cols = piece * n_r
    wide = vecs + PAD
    part = piece * wide
    r = lax.axis_index("row")
    c = lax.axis_index("col")
    core = r % 2
    i = (r // 2) % inner
    o = r // (2 * inner)

    def row_of(oo, ii, cc):
        return (oo * inner + ii) * 2 + cc

    partner = (row_of(o, i, 1 - core), c)
    z_far = [(o + d) % outer for d in range(1, outer)]
    z_src = [(o - d + outer) % outer for d in range(1, outer)]
    x_far = [(i + d) % inner for d in range(1, inner)]
    x_src = [(i - d + inner) % inner for d in range(1, inner)]
    y_far = [(c + d) % n_c for d in range(1, n_c)]
    y_src = [(c - d + n_c) % n_c for d in range(1, n_c)]

    def tile_copy(ch):
        at = pl.ds(ch * step, step)
        return pltpu.make_async_copy(tiles.at[0, 0, at], tbuf.at[at], tile_sem.at[ch])

    for ch in range(chunks):
        tile_copy(ch).start()

    barrier = pltpu.get_barrier_semaphore()
    near = [
        ((i + d) % inner, (core + e) % 2, (i - d + inner) % inner)
        for d in range(inner)
        for e in range(2)
        if d or e
    ]
    wide_set = [
        ((o + d) % outer, (c + e) % n_c, (o - d + outer) % outer, (c - e + n_c) % n_c)
        for d in range(outer)
        for e in range(n_c)
        if d or e
    ]
    near_peers = [(row_of(o, x, cc), c) for x, cc, _ in near]
    near_src = [x * 2 + cc for _, cc, x in near]
    wide_peers = [(row_of(z, i, core), y) for z, y, _, _ in wide_set]
    wide_src = [z * n_c + y for _, _, z, y in wide_set]
    peers = near_peers + wide_peers
    for peer in peers:
        pl.semaphore_signal(barrier, inc=1, device_id=peer, device_id_type=MESH)
    pl.semaphore_wait(barrier, len(peers))

    sent = []

    def send(src, dst, sem, peer):
        copy = pltpu.make_async_remote_copy(
            src_ref=src,
            dst_ref=dst,
            send_sem=send_sem.at[len(sent)],
            recv_sem=sem,
            device_id=peer,
            device_id_type=MESH,
        )
        copy.start()
        sent.append(copy)

    def landed(ref, sem):
        pltpu.make_async_remote_copy(
            src_ref=ref,
            dst_ref=ref,
            send_sem=send_sem.at[0],
            recv_sem=sem,
            device_id=partner,
            device_id_type=MESH,
        ).wait_recv()

    def cv_at(rr):
        return cv.at[pl.ds(rr * piece, piece)]

    def rv_at(cc):
        return rv.at[pl.ds(cc * piece, piece)]

    for y in y_far:
        send(left, rv_at(c), left_sem.at[c], (r, y))
    for z in z_far:
        send(right, cv_at(r), right_sem.at[r], (row_of(z, i, core), c))
    for x in x_far:
        send(right, cv_at(r), right_sem.at[r], (row_of(o, x, core), c))
    send(right, cv_at(r), right_sem.at[r], partner)
    cv[pl.ds(r * piece, piece)] = right[...]
    rv[pl.ds(c * piece, piece)] = left[...]

    def relay_z():
        for z in z_src:
            got = row_of(z, i, core)
            landed(cv_at(got), right_sem.at[got])
            for x in x_far:
                send(cv_at(got), cv_at(got), right_sem.at[got], (row_of(o, x, core), c))
            send(cv_at(got), cv_at(got), right_sem.at[got], partner)

    def relay_x():
        for z in [o] + z_src:
            for x in x_src:
                got = row_of(z, x, core)
                landed(cv_at(got), right_sem.at[got])
                send(cv_at(got), cv_at(got), right_sem.at[got], partner)

    def take_core():
        for z in [o] + z_src:
            for x in [i] + x_src:
                got = row_of(z, x, 1 - core)
                landed(cv_at(got), right_sem.at[got])

    def images(ch, vec_ref, index, limit, turned):
        def body(g, carry):
            for u in range(0, GROUP, PAIR):
                s = ch * step + g * GROUP + u
                xs = [vec_ref[jnp.minimum(index[s + q], limit - 1)] for q in range(PAIR)]
                ts = [tbuf[s + q] for q in range(PAIR)]
                dims = across if turned else plain
                got = mul(jnp.concatenate(xs, 0), jnp.concatenate(ts, 0 if turned else 1), dims)
                for q in range(PAIR):
                    block = got[q * vecs : (q + 1) * vecs, q * side : (q + 1) * side]
                    prod[pl.ds((s + q) * wide, vecs), :] = block
            return carry

        lax.fori_loop(0, step // GROUP, body, 0)

    plain = (((1,), (0,)), ((), ()))
    across = (((1,), (1,)), ((), ()))

    def gather_sums(index_v, rows, target):
        pick = lax.broadcasted_iota(jnp.int32, (rows, slots), 0) == index_v[...]
        pick = jnp.where(pick, 1.0, 0.0).astype(BF16)
        pick = jnp.concatenate([pick, pick], 1)

        def body(g, carry):
            for u in range(0, KGROUP, PAIR):
                k = g * KGROUP + u
                terms = [split(prod[pl.ds(k + q, slots, stride=wide), :]) for q in range(PAIR)]
                high = jnp.concatenate([t[0] for t in terms], 1)
                low = jnp.concatenate([t[1] for t in terms], 1)
                got = mul(pick, jnp.concatenate([high, low], 0))
                for q in range(PAIR):
                    block = got[:, q * side : (q + 1) * side]
                    target[pl.ds(k + q, rows, stride=wide), :] = block
            return carry

        lax.fori_loop(0, vecs // KGROUP, body, 0)

    for y in y_src:
        landed(rv_at(y), left_sem.at[y])
    for ch in range(chunks):
        tile_copy(ch).wait()
        images(ch, rv, row_s, block_rows, False)
    relay_z()
    gather_sums(col_v, block_cols, zp)

    z_order = list(zip(z_far, range(1, outer))) + [(o, 0)]
    x_order = list(zip(x_far, range(1, inner))) + [(i, 0)]
    for z, _ in z_order:
        for x, _ in x_order:
            at = pl.ds(row_of(z, x, 1 - core) * part, part)
            slot = z * inner + x
            send(zp.at[at], zc.at[slot], zc_sem.at[slot], partner)
    relay_x()
    take_core()

    def gram_step(p, total):
        sums, mates = [], []
        for t in range(piece):
            high, low = split(zp[pl.ds(p * part + t * wide, vecs), :])
            sums.append(jnp.concatenate([high, low], 0))
            mates.append(cv[p * piece + t])
        return total + mul(jnp.concatenate(sums, 1), jnp.concatenate(mates, 1), across)

    total = lax.fori_loop(0, n_r, gram_step, jnp.zeros((2 * vecs, vecs), F32))

    def spread(value, buf, base, me, far):
        buf[me] = value
        for peer in far:
            send(buf.at[me], buf.at[me], g_sem.at[base + me], peer)

    def collect(buf, base, src):
        for q in src:
            landed(buf.at[q], g_sem.at[base + q])
        total = buf[0]
        for q in range(1, buf.shape[0]):
            total = total + buf[q]
        return total

    spread(total[:vecs] + total[vecs:], ga, 0, i * 2 + core, near_peers)
    def encode(block_of, q_ref, s_ref):
        scales = []
        for t in range(piece):
            block = block_of(t)
            top = jnp.maximum(jnp.max(jnp.abs(block), axis=0, keepdims=True), LEAST)
            q_ref[t * vecs : (t + 1) * vecs] = (
                jnp.round(block * (TOP / top)).astype(jnp.int32).astype(jnp.int16)
            )
            scales.append(top * (1.0 / TOP))
        s_ref[...] = jnp.concatenate(scales, 0)

    def decode(q_ref, s_ref, t):
        code = q_ref[t * vecs : (t + 1) * vecs].astype(jnp.int32).astype(F32)
        return code * s_ref[t : t + 1]

    def pair_sum(z, x, t):
        mine = zp[pl.ds(row_of(z, x, core) * part + t * wide, vecs), :]
        return mine + zc[z * inner + x, t * wide : t * wide + vecs]

    for z, _ in z_order:
        for x, dx in x_order:
            slot = z * inner + x
            landed(zc.at[slot], zc_sem.at[slot])
            if dx:
                encode(functools.partial(pair_sum, z, x), qx_out.at[dx - 1, z], sx_out.at[dx - 1, z])
                peer = (row_of(o, x, core), c)
                send(qx_out.at[dx - 1, z], qx.at[dx - 1, z], zx_sem.at[dx - 1, z], peer)
                send(sx_out.at[dx - 1, z], sx.at[dx - 1, z], sx_sem.at[dx - 1, z], peer)
    for ch in range(chunks // 2):
        images(ch, cv, col_s, block_cols, True)
    spread(collect(ga, 0, near_src), gb, 2 * inner, o * n_c + c, wide_peers)
    for ch in range(chunks // 2, chunks):
        images(ch, cv, col_s, block_cols, True)
    gather_sums(row_v, block_rows, yp)
    for y in y_far:
        dy = (y - c + n_c) % n_c
        send(yp.at[pl.ds(y * part, part)], yl.at[dy], y_sem.at[dy], (r, y))

    def plane_sum(z, t):
        total = pair_sum(z, i, t)
        for d in range(1, inner):
            total = total + decode(qx.at[d - 1, z], sx.at[d - 1, z], t)
        return total

    for z, dz in z_order:
        for d in range(1, inner):
            landed(qx.at[d - 1, z], zx_sem.at[d - 1, z])
            landed(sx.at[d - 1, z], sx_sem.at[d - 1, z])
        if dz:
            encode(functools.partial(plane_sum, z), qz_out.at[dz - 1], sz_out.at[dz - 1])
            peer = (row_of(z, i, core), c)
            send(qz_out.at[dz - 1], qz.at[dz - 1], zz_sem.at[dz - 1], peer)
            send(sz_out.at[dz - 1], sz.at[dz - 1], sz_sem.at[dz - 1], peer)
        else:
            for t in range(piece):
                zs[t * vecs : (t + 1) * vecs] = plane_sum(z, t)

    gram = collect(gb, 2 * inner, wide_src)
    gram = gram * (block_cols * n_c * side) ** (-0.5)
    out_g[...] = gram
    y_total = yp[pl.ds(c * part, part), :]
    for d in range(1, n_c):
        landed(yl.at[d], y_sem.at[d])
        y_total = y_total + yl[d]
    out_y[...] = y_total
    for d in range(1, outer):
        landed(qz.at[d - 1], zz_sem.at[d - 1])
        landed(sz.at[d - 1], sz_sem.at[d - 1])
    for t in range(piece):
        total = zs[t * vecs : (t + 1) * vecs]
        for d in range(1, outer):
            total = total + decode(qz.at[d - 1], sz.at[d - 1], t)
        out_z[t] = total
    for copy in sent:
        copy.wait_send()


def finish(y_ref, z_ref, gram_ref, right, left, out_r, out_l, out_g):
    piece, vecs, _ = right.shape
    wide = y_ref.shape[0] // piece
    gram = gram_ref[...]
    out_g[...] = gram
    high, low = split(gram)
    turned_high, turned_low = split(gram.T)
    for t in range(piece):
        at = slice(t * wide, t * wide + vecs)
        out_r[t] = y_ref[at] - (mul(turned_high, right[t]) + mul(turned_low, right[t]))
        out_l[t] = z_ref[t] - (mul(high, left[t]) + mul(low, left[t]))


def solution(mesh):
    n_r, n_c = mesh.shape["row"], mesh.shape["col"]
    half = n_r // 2
    inner = 1 << ((half.bit_length() - 1) // 2)
    outer = half // inner

    def per_device(tiles, tile_row, tile_col, right_vecs, left_vecs):
        slots, side = tiles.shape[2], tiles.shape[3]
        piece, vecs, _ = right_vecs.shape
        chunks = 8
        wide = vecs + PAD
        part = piece * wide
        block_rows, block_cols = piece * n_c, piece * n_r
        planes = outer * inner
        near, far = max(inner - 1, 1), max(outer - 1, 1)
        sends = (
            2 * (n_c - 1)
            + (outer - 1)
            + (inner - 1)
            + 1
            + (outer - 1) * inner
            + outer * (inner - 1)
            + planes
            + 2 * outer * (inner - 1)
            + 2 * (outer - 1)
            + (2 * inner - 1)
            + (outer * n_c - 1)
        )
        vmem = pl.BlockSpec(memory_space=pltpu.VMEM)
        smem = pl.BlockSpec(memory_space=pltpu.SMEM)
        dma = pltpu.SemaphoreType.DMA
        row_s = tile_row.reshape(slots)
        col_s = tile_col.reshape(slots)
        y_total, z_total, gram = pl.pallas_call(
            functools.partial(kernel, (n_r, n_c, outer, inner, chunks)),
            out_shape=(
                jax.ShapeDtypeStruct((part, side), F32),
                jax.ShapeDtypeStruct((piece, vecs, side), F32),
                jax.ShapeDtypeStruct((vecs, vecs), F32),
            ),
            in_specs=[smem, smem, vmem, vmem, vmem, vmem, pl.BlockSpec(memory_space=pl.ANY)],
            out_specs=(vmem, vmem, vmem),
            scratch_shapes=[
                pltpu.VMEM((slots, side, side), BF16),
                pltpu.VMEM((block_cols, vecs, side), BF16),
                pltpu.VMEM((block_rows, vecs, side), BF16),
                pltpu.VMEM((slots * wide, side), F32),
                pltpu.VMEM((block_cols * wide, side), F32),
                pltpu.VMEM((planes, part, side), F32),
                pltpu.VMEM((piece * vecs, side), F32),
                *[
                    pltpu.VMEM(lead + shape, kind)
                    for lead in [(near, outer)] * 2 + [(far,)] * 2
                    for shape, kind in [((piece * vecs, side), jnp.int16), ((piece, side), F32)]
                ],
                pltpu.VMEM((block_rows * wide, side), F32),
                pltpu.VMEM((n_c, part, side), F32),
                pltpu.VMEM((2 * inner, vecs, vecs), F32),
                pltpu.VMEM((outer * n_c, vecs, vecs), F32),
                dma((chunks,)),
                dma((sends,)),
                dma((n_c,)),
                dma((n_r,)),
                dma((planes,)),
                *[dma((near, outer)), dma((far,))] * 2,
                dma((n_c,)),
                dma((2 * inner + outer * n_c,)),
            ],
            compiler_params=pltpu.CompilerParams(
                collective_id=0, has_side_effects=True, vmem_limit_bytes=60 * 1024 * 1024
            ),
            name="arnoldi_step",
        )(row_s, col_s, row_s.reshape(1, slots), col_s.reshape(1, slots), right_vecs, left_vecs, tiles)
        return pl.pallas_call(
            finish,
            out_shape=(
                jax.ShapeDtypeStruct((piece, vecs, side), F32),
                jax.ShapeDtypeStruct((piece, vecs, side), F32),
                jax.ShapeDtypeStruct((vecs, vecs), F32),
            ),
            in_specs=[vmem] * 5,
            out_specs=(vmem, vmem, vmem),
            name="finish",
        )(y_total, z_total, gram, right_vecs, left_vecs)

    placed = (
        P("row", "col", None, None, None),
        P("row", "col", None),
        P("row", "col", None),
        P(("row", "col"), None, None),
        P(("row", "col"), None, None),
    )
    return jax.shard_map(
        per_device,
        mesh=mesh,
        in_specs=placed,
        out_specs=(P(("row", "col"), None, None), P(("row", "col"), None, None), P()),
        check_vma=False,
    )
```

profile of v0, /device:TPU:0, one launch (start us, length us, event | category | flops | bytes accessed | tf_op | source)
XLA Modules:
  0.0 37.8 jit_solution(14670609294820086670)
XLA Ops:
  0.6 35.2 %arnoldi_step.1 = (f32[264,128]{1,0:T(8,128)}, f32[8,32,128]{2,1,0:T(8,128)}, f32[32,32]{1,0:T(8,128)}) custom-call(s32[256]{0:T(256)} %bitcast.4, s32[256]{0:T(256)} %bitcast.6, s32[1,256]{1,0:T(1,128)} %bitcast.5, s32[1,256]{1,0:T(1,128)} %bitcast.7, bf16[8,32,128]{2,1,0:T(8,128)(2,1)} %right.3, bf16[8,32,128]{2,1,0:T(8,128)(2,1)} %left.3, ...), custom_call_target="tpu_custom_call" | custom-call | tf_op jit(solution)/shard_map/arnoldi_step/pallas_call | solution.py:391
  35.8 2.0 %finish.1 = (f32[8,32,128]{2,1,0:T(8,128)}, f32[8,32,128]{2,1,0:T(8,128)}, f32[32,32]{1,0:T(8,128)}) custom-call(f32[264,128]{1,0:T(8,128)} %get-tuple-element.6.y_ref, f32[8,32,128]{2,1,0:T(8,128)} %get-tuple-element.7.z_ref, f32[32,32]{1,0:T(8,128)} %get-tuple-element.8.gram_ref, bf16[8,32,128]{2,1,0:T(8,128)(2,1)} %right.3, bf16[8,32,128]{2,1,0:T(8,128)(2,1)} %left.3), custom_call_target="tpu_custom_call" | custom-call | tf_op jit(solution)/shard_map/finish/pallas_call | solution.py:431
where the time goes:
time: 38 us; the launch traced here: 37.8 us
  Pallas kernels  37.2 us (98%)
  between operations  0.64 us (2%)
    pallas_call x1, Pallas kernels, per_device(): pl.pallas_call(functools.partial(kernel, (n_r, n_c, outer, inner, chunks)...  35.2 us
    pallas_call x1, Pallas kernels, per_device(): pl.pallas_call(finish, out_shape=(jax.ShapeDtypeStruct((piece, vecs, side...  1.95 us

commit v1 on v0

v1 whole, which is shorter than its diff:
```python
import functools
from contextlib import nullcontext as scope

import jax
import jax.numpy as jnp
from jax import lax
from jax.experimental import pallas as pl
from jax.experimental.pallas import tpu as pltpu
from jax.sharding import PartitionSpec as P

MESH = pl.DeviceIdType.MESH
F32 = jnp.float32
BF16 = jnp.bfloat16
GROUP = 32
PAIR = 2
KGROUP = 8
TOP = 32767.0
LEAST = 2.0**-110
PAD = 1


def split(value):
    high = value.astype(BF16)
    low = (value - high.astype(F32)).astype(BF16)
    return high, low


def mul(a, b, dims=(((1,), (0,)), ((), ()))):
    return lax.dot_general(a, b, dims, preferred_element_type=F32)


def flip(at, d, size):
    total, bit = 0, 1
    while bit < size:
        digit = at // bit % 2
        total = total + bit * (1 - digit if d & bit else digit)
        bit *= 2
    return total


def kernel(
    sizes,
    row_at,
    col_at,
    right,
    left,
    tiles,
    out_y,
    out_z,
    out_g,
    tbuf,
    cv,
    rv,
    prod,
    zp,
    zc,
    zs,
    qx_out,
    sx_out,
    qx,
    sx,
    qz_out,
    sz_out,
    qz,
    sz,
    yp,
    qy_out,
    sy_out,
    qy,
    sy,
    ga,
    gb,
    row_s,
    col_s,
    row_v,
    col_v,
    own_sem,
    tile_sem,
    send_sem,
    left_sem,
    right_sem,
    zc_sem,
    zx_sem,
    sx_sem,
    zz_sem,
    sz_sem,
    zy_sem,
    sy_sem,
    g_sem,
):
    n_r, n_c, outer, inner, chunks = sizes
    piece, vecs, side = right.shape
    slots = tbuf.shape[0]
    step = slots // chunks
    block_rows = piece * n_c
    block_cols = piece * n_r
    wide = vecs + PAD
    part = piece * wide
    r = lax.axis_index("row")
    c = lax.axis_index("col")
    core = r % 2
    i = (r // 2) % inner
    o = r // (2 * inner)

    def row_of(oo, ii, cc):
        return (oo * inner + ii) * 2 + cc

    partner = (row_of(o, i, 1 - core), c)
    zs_of = [flip(o, d, outer) for d in range(outer)]
    xs_of = [flip(i, d, inner) for d in range(inner)]
    y_far = [(c + d) % n_c for d in range(1, n_c)]
    y_src = [(c - d + n_c) % n_c for d in range(1, n_c)]

    def tile_copy(ch):
        at = pl.ds(ch * step, step)
        return pltpu.make_async_copy(tiles.at[0, 0, at], tbuf.at[at], tile_sem.at[ch])

    own = [
        pltpu.make_async_copy(src, dst, own_sem.at[q])
        for q, (src, dst) in enumerate(
            [
                (right, cv.at[pl.ds(r * piece, piece)]),
                (left, rv.at[pl.ds(c * piece, piece)]),
                (row_at, row_s),
                (col_at, col_s),
                (row_at, row_v),
                (col_at, col_v),
            ]
        )
    ]
    for copy in own:
        copy.start()

    barrier = pltpu.get_barrier_semaphore()
    near = [
        ((i + d) % inner, (core + e) % 2, (i - d + inner) % inner)
        for d in range(inner)
        for e in range(2)
        if d or e
    ]
    wide_set = [
        ((o + d) % outer, (c + e) % n_c, (o - d + outer) % outer, (c - e + n_c) % n_c)
        for d in range(outer)
        for e in range(n_c)
        if d or e
    ]
    near_peers = [(row_of(o, x, cc), c) for x, cc, _ in near]
    near_src = [x * 2 + cc for _, cc, x in near]
    wide_peers = [(row_of(z, i, core), y) for z, y, _, _ in wide_set]
    wide_src = [z * n_c + y for _, _, z, y in wide_set]
    peers = near_peers + wide_peers
    for peer in peers:
        pl.semaphore_signal(barrier, inc=1, device_id=peer, device_id_type=MESH)
    pl.semaphore_wait(barrier, len(peers))

    sent = []

    def send(src, dst, sem, peer):
        copy = pltpu.make_async_remote_copy(
            src_ref=src,
            dst_ref=dst,
            send_sem=send_sem.at[len(sent)],
            recv_sem=sem,
            device_id=peer,
            device_id_type=MESH,
        )
        copy.start()
        sent.append(copy)

    def landed(ref, sem):
        pltpu.make_async_remote_copy(
            src_ref=ref,
            dst_ref=ref,
            send_sem=send_sem.at[0],
            recv_sem=sem,
            device_id=partner,
            device_id_type=MESH,
        ).wait_recv()

    def cv_at(rr):
        return cv.at[pl.ds(rr * piece, piece)]

    def rv_at(cc):
        return rv.at[pl.ds(cc * piece, piece)]

    for y in y_far:
        send(left, rv_at(c), left_sem.at[c], (r, y))
    for x in xs_of[1:]:
        send(right, cv_at(r), right_sem.at[r], (row_of(o, x, core), c))
    for z in zs_of[1:]:
        send(right, cv_at(r), right_sem.at[r], (row_of(z, i, core), c))
    send(right, cv_at(r), right_sem.at[r], partner)
    for ch in range(chunks):
        tile_copy(ch).start()

    def take_z(d):
        with scope("take_z%d" % d):
            got = row_of(zs_of[d], i, core)
            landed(cv_at(got), right_sem.at[got])
            for x in xs_of[1:]:
                send(cv_at(got), cv_at(got), right_sem.at[got], (row_of(o, x, core), c))
            send(cv_at(got), cv_at(got), right_sem.at[got], partner)

    def take_x(d):
        with scope("take_x%d" % d):
            for x in xs_of[1:]:
                got = row_of(zs_of[d], x, core)
                landed(cv_at(got), right_sem.at[got])
                send(cv_at(got), cv_at(got), right_sem.at[got], partner)

    def take_core(d):
        with scope("take_c%d" % d):
            for x in xs_of:
                got = row_of(zs_of[d], x, 1 - core)
                landed(cv_at(got), right_sem.at[got])

    def images(ch, vec_ref, index, limit, turned):
        def body(g, carry):
            for u in range(0, GROUP, PAIR):
                s = ch * step + g * GROUP + u
                xs = [vec_ref[jnp.minimum(index[0, s + q], limit - 1)] for q in range(PAIR)]
                ts = [tbuf[s + q] for q in range(PAIR)]
                dims = across if turned else plain
                got = mul(jnp.concatenate(xs, 0), jnp.concatenate(ts, 0 if turned else 1), dims)
                for q in range(PAIR):
                    block = got[q * vecs : (q + 1) * vecs, q * side : (q + 1) * side]
                    prod[pl.ds((s + q) * wide, vecs), :] = block
            return carry

        lax.fori_loop(0, step // GROUP, body, 0)

    plain = (((1,), (0,)), ((), ()))
    across = (((1,), (1,)), ((), ()))

    def gather_sums(index_v, rows, target, first=0, last=vecs // KGROUP):
        pick = lax.broadcasted_iota(jnp.int32, (rows, slots), 0) == index_v[...]
        pick = jnp.where(pick, 1.0, 0.0).astype(BF16)
        pick = jnp.concatenate([pick, pick], 1)

        def body(g, carry):
            for u in range(0, KGROUP, PAIR):
                k = g * KGROUP + u
                terms = [split(prod[pl.ds(k + q, slots, stride=wide), :]) for q in range(PAIR)]
                high = jnp.concatenate([t[0] for t in terms], 1)
                low = jnp.concatenate([t[1] for t in terms], 1)
                got = mul(pick, jnp.concatenate([high, low], 0))
                for q in range(PAIR):
                    block = got[:, q * side : (q + 1) * side]
                    target[pl.ds(k + q, rows, stride=wide), :] = block
            return carry

        lax.fori_loop(first, last, body, 0)

    def encode(block_of, q_ref, s_ref):
        scales = []
        for t in range(piece):
            block = block_of(t)
            top = jnp.maximum(jnp.max(jnp.abs(block), axis=0, keepdims=True), LEAST)
            q_ref[t * vecs : (t + 1) * vecs] = (
                jnp.round(block * (TOP / top)).astype(jnp.int32).astype(jnp.int16)
            )
            scales.append(top * (1.0 / TOP))
        s_ref[...] = jnp.concatenate(scales, 0)

    def decode(q_ref, s_ref, t):
        code = q_ref[t * vecs : (t + 1) * vecs].astype(jnp.int32).astype(F32)
        return code * s_ref[t : t + 1]

    def pair_sum(dz, dx, t):
        at = row_of(zs_of[dz], xs_of[dx], core) * part + t * wide
        return zp[pl.ds(at, vecs), :] + zc[dz * inner + dx, t * wide : t * wide + vecs]

    def give_core():
        with scope("give_core"):
            for dx in range(inner - 1, -1, -1):
                for dz in range(outer - 1, -1, -1):
                    at = pl.ds(row_of(zs_of[dz], xs_of[dx], 1 - core) * part, part)
                    slot = dz * inner + dx
                    send(zp.at[at], zc.at[slot], zc_sem.at[slot], partner)

    def give_x(dz):
        with scope("give_x%d" % dz):
            for dx in range(inner - 1, 0, -1):
                slot = dz * inner + dx
                landed(zc.at[slot], zc_sem.at[slot])
                out = qx_out.at[dx - 1, dz], sx_out.at[dx - 1, dz]
                encode(functools.partial(pair_sum, dz, dx), *out)
                peer = (row_of(o, xs_of[dx], core), c)
                send(out[0], qx.at[dx - 1, dz], zx_sem.at[dx - 1, dz], peer)
                send(out[1], sx.at[dx - 1, dz], sx_sem.at[dx - 1, dz], peer)

    def own_x():
        with scope("own_x"):
            for dz in range(outer - 1, -1, -1):
                landed(zc.at[dz * inner], zc_sem.at[dz * inner])

    def plane_sum(dz, t):
        total = pair_sum(dz, 0, t)
        for d in range(1, inner):
            total = total + decode(qx.at[d - 1, dz], sx.at[d - 1, dz], t)
        return total

    def give_z(dz):
        with scope("give_z%d" % dz):
            for d in range(1, inner):
                landed(qx.at[d - 1, dz], zx_sem.at[d - 1, dz])
                landed(sx.at[d - 1, dz], sx_sem.at[d - 1, dz])
            if dz:
                out = qz_out.at[dz - 1], sz_out.at[dz - 1]
                encode(functools.partial(plane_sum, dz), *out)
                peer = (row_of(zs_of[dz], i, core), c)
                send(out[0], qz.at[dz - 1], zz_sem.at[dz - 1], peer)
                send(out[1], sz.at[dz - 1], sz_sem.at[dz - 1], peer)
            else:
                for t in range(piece):
                    zs[t * vecs : (t + 1) * vecs] = plane_sum(0, t)

    def gram_plane(d, total):
        with scope("gram%d" % d):
            sums, mates = [], []
            for dx in range(inner):
                p = row_of(zs_of[d], xs_of[dx], core)
                for t in range(piece):
                    high, low = split(pair_sum(d, dx, t))
                    sums.append(jnp.concatenate([high, low], 0))
                    mates.append(cv[p * piece + t])
            return total + mul(jnp.concatenate(sums, 1), jnp.concatenate(mates, 1), across)

    def spread(value, buf, base, me, far):
        with scope("spread%d" % base):
            buf[me] = value
            for peer in far:
                send(buf.at[me], buf.at[me], g_sem.at[base + me], peer)

    def collect(buf, base, src):
        with scope("collect%d" % base):
            for q in src:
                landed(buf.at[q], g_sem.at[base + q])
            total = buf[0]
            for q in range(1, buf.shape[0]):
                total = total + buf[q]
            return total

    with scope("wait_left"):
        for copy in own:
            copy.wait()
        for y in y_src:
            landed(rv_at(y), left_sem.at[y])

    def left_images(first, last):
        with scope("imgL%d" % first):
            for ch in range(first, last):
                tile_copy(ch).wait()
                images(ch, rv, row_s, block_rows, False)

    def right_images(first, last):
        with scope("imgR%d" % first):
            for ch in range(first, last):
                images(ch, cv, col_s, block_cols, True)

    later = list(range(1, outer))
    groups = vecs // KGROUP
    left_images(0, 3)
    take_z(1)
    take_x(0)
    left_images(3, 6)
    for d in later[1:-1]:
        take_z(d)
    left_images(6, chunks)
    take_z(later[-1])
    with scope("gatherZ"):
        gather_sums(col_v, block_cols, zp)
    give_core()
    take_x(1)
    for d in later[::-1]:
        give_x(d)
    give_x(0)
    own_x()
    total = gram_plane(0, jnp.zeros((2 * vecs, vecs), F32))
    total = gram_plane(1, total)
    for d in later[1:]:
        take_x(d)
        total = gram_plane(d, total)
    spread(total[:vecs] + total[vecs:], gb, 2 * inner, o * n_c + c, wide_peers)
    for d in range(outer):
        take_core(d)

    right_images(0, 2)
    give_z(later[-1])
    right_images(2, 4)
    for d in later[-2:0:-1]:
        give_z(d)
    right_images(4, 6)
    give_z(later[0])
    right_images(6, chunks)
    with scope("gatherY"):
        gather_sums(row_v, block_rows, yp)
    with scope("give_y"):
        for d, y in enumerate(y_far):
            encode(lambda t: yp[pl.ds(y * part + t * wide, vecs), :], qy_out.at[d], sy_out.at[d])
            send(qy_out.at[d], qy.at[d], zy_sem.at[d], (r, y))
            send(sy_out.at[d], sy.at[d], sy_sem.at[d], (r, y))
    give_z(0)
    spread(collect(gb, 2 * inner, wide_src), ga, 0, i * 2 + core, near_peers)
    gram = collect(ga, 0, near_src)
    gram = gram * (block_cols * n_c * side) ** (-0.5)
    out_g[...] = gram
    with scope("wait_y"):
        for d in range(n_c - 1):
            landed(qy.at[d], zy_sem.at[d])
            landed(sy.at[d], sy_sem.at[d])
    with scope("out_y"):
        for t in range(piece):
            total = yp[pl.ds(c * part + t * wide, vecs), :]
            for d in range(n_c - 1):
                total = total + decode(qy.at[d], sy.at[d], t)
            out_y[t] = total
    with scope("wait_z"):
        for d in range(1, outer):
            landed(qz.at[d - 1], zz_sem.at[d - 1])
            landed(sz.at[d - 1], sz_sem.at[d - 1])
    with scope("out_z"):
        for t in range(piece):
            total = zs[t * vecs : (t + 1) * vecs]
            for d in range(1, outer):
                total = total + decode(qz.at[d - 1], sz.at[d - 1], t)
            out_z[t] = total
    with scope("wait_send"):
        for copy in sent:
            copy.wait_send()


def finish(y_ref, z_ref, gram_ref, right, left, out_r, out_l, out_g):
    piece, vecs, _ = right.shape
    gram = gram_ref[...]
    out_g[...] = gram
    high, low = split(gram)
    turned_high, turned_low = split(gram.T)
    for t in range(piece):
        out_r[t] = y_ref[t] - (mul(turned_high, right[t]) + mul(turned_low, right[t]))
        out_l[t] = z_ref[t] - (mul(high, left[t]) + mul(low, left[t]))


def solution(mesh):
    n_r, n_c = mesh.shape["row"], mesh.shape["col"]
    half = n_r // 2
    inner = 1 << ((half.bit_length() - 1) // 2)
    outer = half // inner

    def per_device(tiles, tile_row, tile_col, right_vecs, left_vecs):
        slots, side = tiles.shape[2], tiles.shape[3]
        piece, vecs, _ = right_vecs.shape
        chunks = 8
        wide = vecs + PAD
        part = piece * wide
        block_rows, block_cols = piece * n_c, piece * n_r
        planes = outer * inner
        near, far, mates = max(inner - 1, 1), max(outer - 1, 1), max(n_c - 1, 1)
        sends = (
            3 * (n_c - 1)
            + (outer - 1)
            + (inner - 1)
            + 1
            + (outer - 1) * inner
            + outer * (inner - 1)
            + planes
            + 2 * outer * (inner - 1)
            + 2 * (outer - 1)
            + (2 * inner - 1)
            + (outer * n_c - 1)
        )
        vmem = pl.BlockSpec(memory_space=pltpu.VMEM)
        dma = pltpu.SemaphoreType.DMA
        y_total, z_total, gram = pl.pallas_call(
            functools.partial(kernel, (n_r, n_c, outer, inner, chunks)),
            out_shape=(
                jax.ShapeDtypeStruct((piece, vecs, side), F32),
                jax.ShapeDtypeStruct((piece, vecs, side), F32),
                jax.ShapeDtypeStruct((vecs, vecs), F32),
            ),
            in_specs=[pl.BlockSpec(memory_space=pl.ANY)] * 5,
            out_specs=(vmem, vmem, vmem),
            scratch_shapes=[
                pltpu.VMEM((slots, side, side), BF16),
                pltpu.VMEM((block_cols, vecs, side), BF16),
                pltpu.VMEM((block_rows, vecs, side), BF16),
                pltpu.VMEM((slots * wide, side), F32),
                pltpu.VMEM((block_cols * wide, side), F32),
                pltpu.VMEM((planes, part, side), F32),
                pltpu.VMEM((piece * vecs, side), F32),
                *[
                    pltpu.VMEM(lead + shape, kind)
                    for lead in [(near, outer)] * 2 + [(far,)] * 2
                    for shape, kind in [((piece * vecs, side), jnp.int16), ((piece, side), F32)]
                ],
                pltpu.VMEM((block_rows * wide, side), F32),
                *[
                    pltpu.VMEM((mates,) + shape, kind)
                    for shape, kind in [((piece * vecs, side), jnp.int16), ((piece, side), F32)] * 2
                ],
                pltpu.VMEM((2 * inner, vecs, vecs), F32),
                pltpu.VMEM((outer * n_c, vecs, vecs), F32),
                *[pltpu.SMEM((1, slots), jnp.int32)] * 2,
                *[pltpu.VMEM((1, slots), jnp.int32)] * 2,
                dma((6,)),
                dma((chunks,)),
                dma((sends,)),
                dma((n_c,)),
                dma((n_r,)),
                dma((planes,)),
                *[dma((near, outer))] * 2,
                *[dma((far,))] * 2,
                *[dma((mates,))] * 2,
                dma((2 * inner + outer * n_c,)),
            ],
            compiler_params=pltpu.CompilerParams(
                collective_id=0, has_side_effects=True, vmem_limit_bytes=60 * 1024 * 1024
            ),
            name="arnoldi_step",
        )(tile_row.reshape(1, slots), tile_col.reshape(1, slots), right_vecs, left_vecs, tiles)
        return pl.pallas_call(
            finish,
            out_shape=(
                jax.ShapeDtypeStruct((piece, vecs, side), F32),
                jax.ShapeDtypeStruct((piece, vecs, side), F32),
                jax.ShapeDtypeStruct((vecs, vecs), F32),
            ),
            in_specs=[vmem] * 5,
            out_specs=(vmem, vmem, vmem),
            name="finish",
        )(y_total, z_total, gram, right_vecs, left_vecs)

    placed = (
        P("row", "col", None, None, None),
        P("row", "col", None),
        P("row", "col", None),
        P(("row", "col"), None, None),
        P(("row", "col"), None, None),
    )
    return jax.shard_map(
        per_device,
        mesh=mesh,
        in_specs=placed,
        out_specs=(P(("row", "col"), None, None), P(("row", "col"), None, None), P()),
        check_vma=False,
    )
```

time: 38 us -> 33.4 us (0.88)
  Pallas kernels: 37.2 us -> 32.6 us
    pallas_call x1, Pallas kernels: 35.2 us -> 30.6 us  [per_device(): pl.pallas_call(functools.partial(kernel, (n_r, n_c, outer, inner, chunks)...]
where the time goes in v1:
time: 33.4 us; the launch traced here: 33.2 us
  Pallas kernels  32.6 us (98%)
  between operations  0.64 us (2%)
    pallas_call x1, Pallas kernels, per_device(): pl.pallas_call(functools.partial(kernel, (n_r, n_c, outer, inner, chunks)...  30.6 us
    pallas_call x1, Pallas kernels, per_device(): pl.pallas_call(finish, out_shape=(jax.ShapeDtypeStruct((piece, vecs, side...  1.95 us

profile of v1, /device:TPU:0, one launch (start us, length us, event | category | flops | bytes accessed | tf_op | source)
XLA Modules:
  0.0 33.2 jit_solution(10852554943414838143)
XLA Ops:
  0.6 30.6 %arnoldi_step.1 = (f32[8,32,128]{2,1,0:T(8,128)}, f32[8,32,128]{2,1,0:T(8,128)}, f32[32,32]{1,0:T(8,128)}) custom-call(s32[1,256]{1,0:T(1,128)} %bitcast.2, s32[1,256]{1,0:T(1,128)} %bitcast.3, bf16[8,32,128]{2,1,0:T(8,128)(2,1)} %right.3, bf16[8,32,128]{2,1,0:T(8,128)(2,1)} %left.3, bf16[1,1,256,128,128]{4,3,2,1,0:T(8,128)(2,1)} %tiles.1), custom_call_target="tpu_custom_call" | custom-call | tf_op jit(solution)/shard_map/arnoldi_step/pallas_call | solution.py:474
  31.3 2.0 %finish.1 = (f32[8,32,128]{2,1,0:T(8,128)}, f32[8,32,128]{2,1,0:T(8,128)}, f32[32,32]{1,0:T(8,128)}) custom-call(f32[8,32,128]{2,1,0:T(8,128)} %get-tuple-element.6.y_ref, f32[8,32,128]{2,1,0:T(8,128)} %get-tuple-element.7.z_ref, f32[32,32]{1,0:T(8,128)} %get-tuple-element.8.gram_ref, bf16[8,32,128]{2,1,0:T(8,128)(2,1)} %right.3, bf16[8,32,128]{2,1,0:T(8,128)(2,1)} %left.3), custom_call_target="tpu_custom_call" | custom-call | tf_op jit(solution)/shard_map/finish/pallas_call | solution.py:521

commit v2 on v1

--- a/solution.py
+++ b/solution.py
@@ -270,10 +270,13 @@
         at = row_of(zs_of[dz], xs_of[dx], core) * part + t * wide
         return zp[pl.ds(at, vecs), :] + zc[dz * inner + dx, t * wide : t * wide + vecs]
 
+    powers = [1 << b for b in range(outer.bit_length() - 1)]
+    z_order = [*range(outer - 1, 0, -2), *range(outer - 2, 0, -2), 0]
+
     def give_core():
         with scope("give_core"):
             for dx in range(inner - 1, -1, -1):
-                for dz in range(outer - 1, -1, -1):
+                for dz in z_order:
                     at = pl.ds(row_of(zs_of[dz], xs_of[dx], 1 - core) * part, part)
                     slot = dz * inner + dx
                     send(zp.at[at], zc.at[slot], zc_sem.at[slot], partner)
@@ -294,26 +297,45 @@
             for dz in range(outer - 1, -1, -1):
                 landed(zc.at[dz * inner], zc_sem.at[dz * inner])
 
+    def low_bit(d):
+        return d & -d
+
+    def merged(dz):
+        return [dz | b for b in powers if b < (low_bit(dz) or outer)]
+
     def plane_sum(dz, t):
         total = pair_sum(dz, 0, t)
         for d in range(1, inner):
             total = total + decode(qx.at[d - 1, dz], sx.at[d - 1, dz], t)
         return total
 
+    def arrived(d):
+        landed(qz.at[d - 1], zz_sem.at[d - 1])
+        landed(sz.at[d - 1], sz_sem.at[d - 1])
+
     def give_z(dz):
         with scope("give_z%d" % dz):
             for d in range(1, inner):
                 landed(qx.at[d - 1, dz], zx_sem.at[d - 1, dz])
                 landed(sx.at[d - 1, dz], sx_sem.at[d - 1, dz])
-            if dz:
-                out = qz_out.at[dz - 1], sz_out.at[dz - 1]
-                encode(functools.partial(plane_sum, dz), *out)
-                peer = (row_of(zs_of[dz], i, core), c)
-                send(out[0], qz.at[dz - 1], zz_sem.at[dz - 1], peer)
-                send(out[1], sz.at[dz - 1], sz_sem.at[dz - 1], peer)
-            else:
+            if dz == 0:
                 for t in range(piece):
                     zs[t * vecs : (t + 1) * vecs] = plane_sum(0, t)
+                return
+            for d in merged(dz):
+                arrived(d)
+
+            def block(t):
+                total = plane_sum(dz, t)
+                for d in merged(dz):
+                    total = total + decode(qz.at[d - 1], sz.at[d - 1], t)
+                return total
+
+            out = qz_out.at[dz - 1], sz_out.at[dz - 1]
+            encode(block, *out)
+            peer = (row_of(zs_of[low_bit(dz)], i, core), c)
+            send(out[0], qz.at[dz - 1], zz_sem.at[dz - 1], peer)
+            send(out[1], sz.at[dz - 1], sz_sem.at[dz - 1], peer)
 
     def gram_plane(d, total):
         with scope("gram%d" % d):
@@ -358,41 +380,47 @@
             for ch in range(first, last):
                 images(ch, cv, col_s, block_cols, True)
 
-    later = list(range(1, outer))
+    def maybe(step, d):
+        if d < outer:
+            step(d)
+
+    left_images(0, 2)
+    maybe(take_z, 1)
+    left_images(2, 5)
+    take_x(0)
+    left_images(5, chunks)
+    maybe(take_z, 2)
     groups = vecs // KGROUP
-    left_images(0, 3)
-    take_z(1)
-    take_x(0)
-    left_images(3, 6)
-    for d in later[1:-1]:
+    with scope("gatherZa"):
+        gather_sums(col_v, block_cols, zp, 0, groups // 2)
+    for d in range(3, outer):
         take_z(d)
-    left_images(6, chunks)
-    take_z(later[-1])
-    with scope("gatherZ"):
-        gather_sums(col_v, block_cols, zp)
+    with scope("gatherZb"):
+        gather_sums(col_v, block_cols, zp, groups // 2, groups)
     give_core()
-    take_x(1)
-    for d in later[::-1]:
+    maybe(take_x, 1)
+    maybe(take_x, 2)
+    for d in z_order:
         give_x(d)
-    give_x(0)
+    for d in range(3, outer):
+        take_x(d)
     own_x()
-    total = gram_plane(0, jnp.zeros((2 * vecs, vecs), F32))
-    total = gram_plane(1, total)
-    for d in later[1:]:
-        take_x(d)
+    total = jnp.zeros((2 * vecs, vecs), F32)
+    for d in range(outer):
         total = gram_plane(d, total)
     spread(total[:vecs] + total[vecs:], gb, 2 * inner, o * n_c + c, wide_peers)
     for d in range(outer):
         take_core(d)
 
-    right_images(0, 2)
-    give_z(later[-1])
-    right_images(2, 4)
-    for d in later[-2:0:-1]:
+    todo = list(z_order)
+    for ch in range(0, chunks, 2):
+        right_images(ch, ch + 2)
+        if todo and todo[0] & 1:
+            give_z(todo.pop(0))
+        if ch + 4 == chunks:
+            spread(collect(gb, 2 * inner, wide_src), ga, 0, i * 2 + core, near_peers)
+    for d in todo[:-1]:
         give_z(d)
-    right_images(4, 6)
-    give_z(later[0])
-    right_images(6, chunks)
     with scope("gatherY"):
         gather_sums(row_v, block_rows, yp)
     with scope("give_y"):
@@ -401,28 +429,36 @@
             send(qy_out.at[d], qy.at[d], zy_sem.at[d], (r, y))
             send(sy_out.at[d], sy.at[d], sy_sem.at[d], (r, y))
     give_z(0)
-    spread(collect(gb, 2 * inner, wide_src), ga, 0, i * 2 + core, near_peers)
     gram = collect(ga, 0, near_src)
-    gram = gram * (block_cols * n_c * side) ** (-0.5)
-    out_g[...] = gram
+    with scope("correct"):
+        gram = gram * (block_cols * n_c * side) ** (-0.5)
+        out_g[...] = gram
+        high, low = split(gram)
+        turned_high, turned_low = split(gram.T)
+        for t in range(piece):
+            mine = cv[r * piece + t]
+            out_y[t] = yp[pl.ds(c * part + t * wide, vecs), :] - (
+                mul(turned_high, mine) + mul(turned_low, mine)
+            )
+            mine = rv[c * piece + t]
+            out_z[t] = zs[t * vecs : (t + 1) * vecs] - (mul(high, mine) + mul(low, mine))
     with scope("wait_y"):
         for d in range(n_c - 1):
             landed(qy.at[d], zy_sem.at[d])
             landed(sy.at[d], sy_sem.at[d])
     with scope("out_y"):
         for t in range(piece):
-            total = yp[pl.ds(c * part + t * wide, vecs), :]
+            total = out_y[t]
             for d in range(n_c - 1):
                 total = total + decode(qy.at[d], sy.at[d], t)
             out_y[t] = total
     with scope("wait_z"):
-        for d in range(1, outer):
-            landed(qz.at[d - 1], zz_sem.at[d - 1])
-            landed(sz.at[d - 1], sz_sem.at[d - 1])
+        for d in powers:
+            arrived(d)
     with scope("out_z"):
         for t in range(piece):
-            total = zs[t * vecs : (t + 1) * vecs]
-            for d in range(1, outer):
+            total = out_z[t]
+            for d in powers:
                 total = total + decode(qz.at[d - 1], sz.at[d - 1], t)
             out_z[t] = total
     with scope("wait_send"):
@@ -430,15 +466,16 @@
             copy.wait_send()
 
 
-def finish(y_ref, z_ref, gram_ref, right, left, out_r, out_l, out_g):
-    piece, vecs, _ = right.shape
-    gram = gram_ref[...]
-    out_g[...] = gram
-    high, low = split(gram)
-    turned_high, turned_low = split(gram.T)
-    for t in range(piece):
-        out_r[t] = y_ref[t] - (mul(turned_high, right[t]) + mul(turned_low, right[t]))
-        out_l[t] = z_ref[t] - (mul(high, left[t]) + mul(low, left[t]))
+def flush(*refs):
+    sem = refs[-1]
+    half = len(refs) // 2
+    copies = [
+        pltpu.make_async_copy(refs[q], refs[half + q], sem.at[q]) for q in range(half)
+    ]
+    for copy in copies:
+        copy.start()
+    for copy in copies:
+        copy.wait()
 
 
 def solution(mesh):
@@ -471,14 +508,11 @@
         )
         vmem = pl.BlockSpec(memory_space=pltpu.VMEM)
         dma = pltpu.SemaphoreType.DMA
-        y_total, z_total, gram = pl.pallas_call(
+        shapes = [(piece, vecs, side), (piece, vecs, side), (vecs, vecs)]
+        held = pl.pallas_call(
             functools.partial(kernel, (n_r, n_c, outer, inner, chunks)),
-            out_shape=(
-                jax.ShapeDtypeStruct((piece, vecs, side), F32),
-                jax.ShapeDtypeStruct((piece, vecs, side), F32),
-                jax.ShapeDtypeStruct((vecs, vecs), F32),
-            ),
-            in_specs=[pl.BlockSpec(memory_space=pl.ANY)] * 5,
+            out_shape=tuple(pltpu.VMEM(shape, F32) for shape in shapes),
+            in_specs=[pl.BlockSpec(memory_space=pltpu.HBM)] * 5,
             out_specs=(vmem, vmem, vmem),
             scratch_shapes=[
                 pltpu.VMEM((slots, side, side), BF16),
@@ -514,21 +548,30 @@
                 dma((2 * inner + outer * n_c,)),
             ],
             compiler_params=pltpu.CompilerParams(
-                collective_id=0, has_side_effects=True, vmem_limit_bytes=60 * 1024 * 1024
+                collective_id=0, has_side_effects=True, vmem_limit_bytes=44 * 1024 * 1024
             ),
             name="arnoldi_step",
-        )(tile_row.reshape(1, slots), tile_col.reshape(1, slots), right_vecs, left_vecs, tiles)
+        )(
+            *[
+                pltpu.with_memory_space_constraint(x, pltpu.HBM)
+                for x in (
+                    tile_row.reshape(1, slots),
+                    tile_col.reshape(1, slots),
+                    right_vecs,
+                    left_vecs,
+                    tiles,
+                )
+            ]
+        )
+        held = [pltpu.with_memory_space_constraint(x, pltpu.VMEM) for x in held]
         return pl.pallas_call(
-            finish,
-            out_shape=(
-                jax.ShapeDtypeStruct((piece, vecs, side), F32),
-                jax.ShapeDtypeStruct((piece, vecs, side), F32),
-                jax.ShapeDtypeStruct((vecs, vecs), F32),
-            ),
-            in_specs=[vmem] * 5,
-            out_specs=(vmem, vmem, vmem),
-            name="finish",
-        )(y_total, z_total, gram, right_vecs, left_vecs)
+            flush,
+            out_shape=tuple(jax.ShapeDtypeStruct(shape, F32) for shape in shapes),
+            in_specs=[vmem] * len(shapes),
+            out_specs=(pl.BlockSpec(memory_space=pl.ANY),) * len(shapes),
+            scratch_shapes=[dma((len(shapes),))],
+            name="flush",
+        )(*held)
 
     placed = (
         P("row", "col", None, None, None),

time: 33.4 us -> 30.7 us (0.919)
  Pallas kernels: 32.6 us -> 29.9 us
    pallas_call x1, Pallas kernels: 30.6 us -> 29.2 us  [per_device(): pl.pallas_call(functools.partial(kernel, (n_r, n_c, outer, inner, chunks)...]
    pallas_call x1, Pallas kernels: 1.95 us -> 0.73 us  [per_device(): pl.pallas_call(flush, out_shape=tuple((jax.ShapeDtypeStruct(shape, F32) f...]
where the time goes in v2:
time: 30.7 us; the launch traced here: 30.5 us
  Pallas kernels  29.9 us (97%)
  between operations  0.64 us (2%)
    pallas_call x1, Pallas kernels, per_device(): pl.pallas_call(functools.partial(kernel, (n_r, n_c, outer, inner, chunks)...  29.2 us
    pallas_call x1, Pallas kernels, per_device(): pl.pallas_call(flush, out_shape=tuple((jax.ShapeDtypeStruct(shape, F32) f...  0.73 us

profile of v2, /device:TPU:0, one launch (start us, length us, event | category | flops | bytes accessed | tf_op | source)
XLA Modules:
  0.0 30.5 jit_solution(2980200341654661161)
XLA Ops:
  0.6 29.2 %arnoldi_step.1 = (f32[8,32,128]{2,1,0:T(8,128)S(1)}, f32[8,32,128]{2,1,0:T(8,128)S(1)}, f32[32,32]{1,0:T(8,128)S(1)}) custom-call(s32[1,256]{1,0:T(1,128)} %bitcast.2, s32[1,256]{1,0:T(1,128)} %bitcast.3, bf16[8,32,128]{2,1,0:T(8,128)(2,1)} %right.1, bf16[8,32,128]{2,1,0:T(8,128)(2,1)} %left.1, bf16[1,1,256,128,128]{4,3,2,1,0:T(8,128)(2,1)} %tiles.1), custom_call_target="tpu_custom_call" | custom-call | tf_op jit(solution)/shard_map/arnoldi_step/pallas_call | solution.py:512
  29.8 0.7 %flush.1 = (f32[8,32,128]{2,1,0:T(8,128)}, f32[8,32,128]{2,1,0:T(8,128)}, f32[32,32]{1,0:T(8,128)}) custom-call(f32[8,32,128]{2,1,0:T(8,128)S(1)} %get-tuple-element.6.refs_0_, f32[8,32,128]{2,1,0:T(8,128)S(1)} %get-tuple-element.7.refs_1_, f32[32,32]{1,0:T(8,128)S(1)} %get-tuple-element.8.refs_2_), custom_call_target="tpu_custom_call" | custom-call | tf_op jit(solution)/shard_map/flush/pallas_call | solution.py:567

commit v3 on v2

v3 whole, which is shorter than its diff:
```python
import functools
from contextlib import nullcontext as scope

import jax
import jax.numpy as jnp
from jax import lax
from jax.experimental import pallas as pl
from jax.experimental.pallas import tpu as pltpu
from jax.sharding import PartitionSpec as P

MESH = pl.DeviceIdType.MESH
F32 = jnp.float32
BF16 = jnp.bfloat16
PAIR = 2
HALVES = 2
TILE_COPIES = 2
RIGHT, LEFT, PAIRED, ALONG_X, ALONG_Z, ALONG_Y, GRAM = range(7)
TOP = 32767.0
LEAST = 2.0**-110
PAD = 1


def split(value):
    high = value.astype(BF16)
    low = (value - high.astype(F32)).astype(BF16)
    return high, low


def mul(a, b, dims=(((1,), (0,)), ((), ()))):
    return lax.dot_general(a, b, dims, preferred_element_type=F32)


def flip(at, d, size):
    total, bit = 0, 1
    while bit < size:
        digit = at // bit % 2
        total = total + bit * (1 - digit if d & bit else digit)
        bit *= 2
    return total


def kernel(
    sizes,
    row_at,
    col_at,
    right,
    left,
    tiles,
    out_y,
    out_z,
    out_g,
    tbuf,
    cv,
    rv,
    prod,
    zp,
    zc,
    zs,
    qx_out,
    sx_out,
    qx,
    sx,
    qz_out,
    sz_out,
    qz,
    sz,
    yp,
    qy_out,
    sy_out,
    qy,
    sy,
    ga,
    gb,
    row_s,
    col_s,
    row_v,
    col_v,
    own_sem,
    tile_sem,
    send_sem,
    left_sem,
    right_sem,
    zc_sem,
    zx_sem,
    zz_sem,
    zy_sem,
    g_sem,
):
    n_r, n_c, outer, inner, chunks = sizes
    piece, vecs, side = right.shape
    slots = tbuf.shape[0]
    step = slots // chunks
    block_rows = piece * n_c
    block_cols = piece * n_r
    wide = vecs + PAD
    part = piece * wide
    r = lax.axis_index("row")
    c = lax.axis_index("col")
    core = r % 2
    i = (r // 2) % inner
    o = r // (2 * inner)

    def row_of(oo, ii, cc):
        return (oo * inner + ii) * 2 + cc

    partner = (row_of(o, i, 1 - core), c)
    zs_of = [flip(o, d, outer) for d in range(outer)]
    xs_of = [flip(i, d, inner) for d in range(inner)]
    y_far = [(c + d) % n_c for d in range(1, n_c)]
    y_src = [(c - d + n_c) % n_c for d in range(1, n_c)]

    def tile_copy(ch):
        at = pl.ds(ch * (slots // TILE_COPIES), slots // TILE_COPIES)
        return pltpu.make_async_copy(tiles.at[0, 0, at], tbuf.at[at], tile_sem.at[ch])

    own = [
        pltpu.make_async_copy(src, dst, own_sem.at[q])
        for q, (src, dst) in enumerate(
            [
                (right, cv.at[pl.ds(r * piece, piece)]),
                (left, rv.at[pl.ds(c * piece, piece)]),
                (row_at, row_s),
                (col_at, col_s),
                (row_at, row_v),
                (col_at, col_v),
            ]
        )
    ]
    for copy in own:
        copy.start()

    barrier = pltpu.get_barrier_semaphore()
    near = [
        ((i + d) % inner, (core + e) % 2)
        for d in range(inner)
        for e in range(2)
        if d or e
    ]
    wide_set = [
        ((o + d) % outer, (c + e) % n_c)
        for d in range(outer)
        for e in range(n_c)
        if d or e
    ]
    near_peers = [(row_of(o, x, cc), c) for x, cc in near]
    wide_peers = [(row_of(z, i, core), y) for z, y in wide_set]
    peers = near_peers + wide_peers
    for peer in peers:
        pl.semaphore_signal(barrier, inc=1, device_id=peer, device_id_type=MESH)
    pl.semaphore_wait(barrier, len(peers))

    def send(src, dst, sem, peer, group):
        pltpu.make_async_remote_copy(
            src_ref=src,
            dst_ref=dst,
            send_sem=send_sem.at[group],
            recv_sem=sem,
            device_id=peer,
            device_id_type=MESH,
        ).start()

    def left_here(ref, group):
        pltpu.make_async_remote_copy(
            src_ref=ref,
            dst_ref=ref,
            send_sem=send_sem.at[group],
            recv_sem=send_sem.at[group],
            device_id=partner,
            device_id_type=MESH,
        ).wait_send()

    def landed(ref, sem):
        pltpu.make_async_remote_copy(
            src_ref=ref,
            dst_ref=ref,
            send_sem=send_sem.at[0],
            recv_sem=sem,
            device_id=partner,
            device_id_type=MESH,
        ).wait_recv()

    def cv_at(rr):
        return cv.at[pl.ds(rr * piece, piece)]

    def rv_at(cc):
        return rv.at[pl.ds(cc * piece, piece)]

    for y in y_far:
        send(left, rv_at(c), left_sem.at[c], (r, y), LEFT)
    for x in xs_of[1:]:
        send(right, cv_at(r), right_sem.at[r], (row_of(o, x, core), c), RIGHT)
    for z in zs_of[1:]:
        send(right, cv_at(r), right_sem.at[r], (row_of(z, i, core), c), RIGHT)
    send(right, cv_at(r), right_sem.at[r], partner, RIGHT)
    for ch in range(TILE_COPIES):
        tile_copy(ch).start()

    def take_z(d):
        with scope("take_z%d" % d):
            got = row_of(zs_of[d], i, core)
            landed(cv_at(got), right_sem.at[got])
            for x in xs_of[1:]:
                send(cv_at(got), cv_at(got), right_sem.at[got], (row_of(o, x, core), c), RIGHT)
            send(cv_at(got), cv_at(got), right_sem.at[got], partner, RIGHT)

    def take_x(d):
        with scope("take_x%d" % d):
            for x in xs_of[1:]:
                got = row_of(zs_of[d], x, core)
                landed(cv_at(got), right_sem.at[got])
                send(cv_at(got), cv_at(got), right_sem.at[got], partner, RIGHT)

    def take_core(d):
        with scope("take_c%d" % d):
            for x in xs_of:
                got = row_of(zs_of[d], x, 1 - core)
                landed(cv_at(got), right_sem.at[got])

    def images(first, last, vec_ref, index, limit, turned):
        for s in range(first * step, last * step, PAIR):
            xs = [vec_ref[jnp.minimum(index[0, s + q], limit - 1)] for q in range(PAIR)]
            ts = [tbuf[s + q] for q in range(PAIR)]
            dims = across if turned else plain
            got = mul(jnp.concatenate(xs, 0), jnp.concatenate(ts, 0 if turned else 1), dims)
            for q in range(PAIR):
                block = got[q * vecs : (q + 1) * vecs, q * side : (q + 1) * side]
                prod[pl.ds((s + q) * wide, vecs), :] = block

    plain = (((1,), (0,)), ((), ()))
    across = (((1,), (1,)), ((), ()))

    def gather_sums(index_v, rows, target, first, last):
        pick = lax.broadcasted_iota(jnp.int32, (rows, slots), 0) == index_v[...]
        pick = jnp.where(pick, 1.0, 0.0).astype(BF16)
        pick = jnp.concatenate([pick, pick], 1)
        for k in range(first, last, PAIR):
            terms = [split(prod[pl.ds(k + q, slots, stride=wide), :]) for q in range(PAIR)]
            high = jnp.concatenate([t[0] for t in terms], 1)
            low = jnp.concatenate([t[1] for t in terms], 1)
            got = mul(pick, jnp.concatenate([high, low], 0))
            for q in range(PAIR):
                block = got[:, q * side : (q + 1) * side]
                target[pl.ds(k + q, rows, stride=wide), :] = block

    def encode(block_of, q_ref, s_ref, rows=vecs):
        scales = []
        for t in range(piece):
            block = block_of(t)
            top = jnp.maximum(jnp.max(jnp.abs(block), axis=0, keepdims=True), LEAST)
            q_ref[t * rows : (t + 1) * rows] = (
                jnp.round(block * (TOP / top)).astype(jnp.int32).astype(jnp.int16)
            )
            scales.append(top * (1.0 / TOP))
        s_ref[...] = jnp.concatenate(scales, 0)

    def decode(q_ref, s_ref, t, rows=vecs):
        code = q_ref[t * rows : (t + 1) * rows].astype(jnp.int32).astype(F32)
        return code * s_ref[t : t + 1]

    def post(out, dst, sem, peer, group, rows=vecs):
        codes = pl.ds(0, piece * rows)
        send(out[0].at[codes], dst[0].at[codes], sem, peer, group)
        send(out[1], dst[1], sem, peer, group)

    def pair_sum(dz, dx, t):
        at = row_of(zs_of[dz], xs_of[dx], core) * part + t * wide
        return zp[pl.ds(at, vecs), :] + zc[dx * outer + dz, t * wide : t * wide + vecs]

    merging, middle = outer == 4, (o + 1) // 2 % 2
    z_order = list(range(outer - 1, -1, -1))

    def give_core():
        with scope("give_core"):
            for dx in range(inner - 1, -1, -1):
                for dz in z_order:
                    at = pl.ds(row_of(zs_of[dz], xs_of[dx], 1 - core) * part, part)
                    slot = dx * outer + dz
                    sem = zc_sem.at[slot - outer + 1 if dx else 0]
                    send(zp.at[at], zc.at[slot], sem, partner, PAIRED)

    def paired(dz):
        for dx in range(1, inner):
            slot = dx * outer + dz
            landed(zc.at[slot], zc_sem.at[slot - outer + 1])

    def give_x(dz):
        with scope("give_x%d" % dz):
            for dx in range(inner - 1, 0, -1):
                out = qx_out.at[dx - 1, dz], sx_out.at[dx - 1, dz]
                encode(functools.partial(pair_sum, dz, dx), *out)
                peer = (row_of(o, xs_of[dx], core), c)
                dst = qx.at[dx - 1, dz], sx.at[dx - 1, dz]
                post(out, dst, zx_sem.at[dx - 1, dz], peer, ALONG_X)

    def own_x():
        with scope("own_x"):
            landed(zc.at[pl.ds(0, outer)], zc_sem.at[0])

    def plane_sum(dz, t):
        total = pair_sum(dz, 0, t)
        for d in range(1, inner):
            total = total + decode(qx.at[d - 1, dz], sx.at[d - 1, dz], t)
        return total

    def arrived(d):
        landed(qz.at[d], zz_sem.at[d])

    def encode_z(dz, extra):
        def block(t):
            total = plane_sum(dz, t)
            for d in extra:
                total = total + decode(qz.at[d], sz.at[d], t)
            return total

        encode(block, qz_out.at[dz - 1], sz_out.at[dz - 1])

    def give_z(dz, extra=()):
        with scope("give_z%d" % dz):
            for d in range(1, inner):
                landed(qx.at[d - 1, dz], zx_sem.at[d - 1, dz])
            if dz == 0:
                for t in range(piece):
                    zs[t * vecs : (t + 1) * vecs] = plane_sum(0, t)
                return
            at, z = dz - 1, zs_of[dz]
            if merging and dz == 3:
                at, z = 3 - middle, zs_of[1] + middle * (zs_of[3] - zs_of[1])
            if extra:
                arrived(extra[0])
            encode_z(dz, extra)
            out = qz_out.at[dz - 1], sz_out.at[dz - 1]
            post(out, (qz.at[at], sz.at[at]), zz_sem.at[at], (row_of(z, i, core), c), ALONG_Z)

    def gram_plane(d, total):
        with scope("gram%d" % d):
            sums, mates = [], []
            for dx in range(inner):
                p = row_of(zs_of[d], xs_of[dx], core)
                for t in range(piece):
                    high, low = split(pair_sum(d, dx, t))
                    sums.append(jnp.concatenate([high, low], 0))
                    mates.append(cv[p * piece + t])
            return total + mul(jnp.concatenate(sums, 1), jnp.concatenate(mates, 1), across)

    def spread(value, buf, stage, me, far):
        with scope("spread%d" % stage):
            buf[me] = value
            for peer in far:
                send(buf.at[me], buf.at[me], g_sem.at[stage], peer, GRAM + stage)

    def collect(buf, stage):
        with scope("collect%d" % stage):
            landed(buf.at[pl.ds(0, buf.shape[0] - 1)], g_sem.at[stage])
            total = buf[0]
            for q in range(1, buf.shape[0]):
                total = total + buf[q]
            return total

    with scope("wait_left"):
        for copy in own:
            copy.wait()
        for y in y_src:
            landed(rv_at(y), left_sem.at[y])

    def left_images(first, last):
        with scope("imgL%d" % first):
            images(first, last, rv, row_s, block_rows, False)

    def right_images(first, last):
        with scope("imgR%d" % first):
            images(first, last, cv, col_s, block_cols, True)

    def maybe(step, d):
        if d < outer:
            step(d)

    maybe(take_z, 1)
    tile_copy(0).wait()
    left_images(0, chunks // 2)
    take_x(0)
    tile_copy(1).wait()
    left_images(chunks // 2, chunks)
    maybe(take_z, 2)
    with scope("gatherZ"):
        gather_sums(col_v, block_cols, zp, 0, vecs)
    for d in range(3, outer):
        take_z(d)
    give_core()
    maybe(take_x, 1)
    todo_x, todo_z = list(z_order), list(z_order)
    paired(todo_x[0])
    give_x(todo_x.pop(0))
    for d in range(2, outer):
        take_x(d)
    for d in todo_x:
        paired(d)
    while len(todo_x) > 2:
        give_x(todo_x.pop(0))
    own_x()
    total = jnp.zeros((2 * vecs, vecs), F32)
    for d in range(outer):
        total = gram_plane(d, total)
    spread(total[:vecs] + total[vecs:], gb, 1, o * n_c + c, wide_peers)
    while len(todo_x) > 1:
        give_x(todo_x.pop(0))
    for d in range(outer):
        take_core(d)
    first = todo_z.pop(0)
    pl.when(core == 0)(lambda: give_z(first))
    right_images(0, 2)
    give_x(todo_x.pop(0))
    pl.when(core == 1)(lambda: give_z(first))
    right_images(2, 5)
    if merging:
        pl.when(middle == 0)(lambda: give_z(2))
        todo_z.remove(2)
    right_images(5, chunks)
    while len(todo_z) > 1:
        give_z(todo_z.pop(0))

    def give_y(h):
        rows = vecs // HALVES
        with scope("gatherY%d" % h):
            gather_sums(row_v, block_rows, yp, h * rows, (h + 1) * rows)
        with scope("give_y%d" % h):
            for d, y in enumerate(y_far):
                out = qy_out.at[d, h], sy_out.at[d, h]
                start = y * part + h * rows
                encode(lambda t: yp[pl.ds(start + t * wide, rows), :], *out, rows)
                dst = qy.at[d, h], sy.at[d, h]
                post(out, dst, zy_sem.at[d, h], (r, y), ALONG_Y, rows)

    for h in range(HALVES):
        give_y(h)
    spread(collect(gb, 1), ga, 0, i * 2 + core, near_peers)
    if merging:
        pl.when(middle == 1)(lambda: give_z(2, [3]))
    give_z(0)
    gram = collect(ga, 0)
    with scope("correct"):
        gram = gram * (block_cols * n_c * side) ** (-0.5)
        out_g[...] = gram
        high, low = split(gram)
        turned_high, turned_low = split(gram.T)
        for t in range(piece):
            mine = cv[r * piece + t]
            out_y[t] = yp[pl.ds(c * part + t * wide, vecs), :] - (
                mul(turned_high, mine) + mul(turned_low, mine)
            )
            mine = rv[c * piece + t]
            out_z[t] = zs[t * vecs : (t + 1) * vecs] - (mul(high, mine) + mul(low, mine))
    for h in range(HALVES):
        rows = vecs // HALVES
        with scope("wait_y%d" % h):
            for d in range(n_c - 1):
                landed(qy.at[d, h], zy_sem.at[d, h])
        for t in range(piece):
            total = out_y[t, h * rows : (h + 1) * rows]
            for d in range(n_c - 1):
                total = total + decode(qy.at[d, h], sy.at[d, h], t, rows)
            out_y[t, h * rows : (h + 1) * rows] = total
    def add_z(slots_in):
        with scope("wait_z"):
            for d in slots_in:
                arrived(d)
        for t in range(piece):
            total = out_z[t]
            for d in slots_in:
                total = total + decode(qz.at[d], sz.at[d], t)
            out_z[t] = total

    if merging:
        pl.when(middle == 1)(lambda: add_z([0, 2, 1]))
        pl.when(middle == 0)(lambda: add_z([0, 1]))
    else:
        add_z(list(range(outer - 1)))
    with scope("wait_send"):
        left_here(cv.at[pl.ds(0, (n_r - 1) * piece)], RIGHT)
        left_here(rv.at[pl.ds(0, (n_c - 1) * piece)], LEFT)
        left_here(zc, PAIRED)
        left_here(qx_out, ALONG_X)
        left_here(qz_out, ALONG_Z)
        left_here(qy_out, ALONG_Y)
        left_here(ga.at[pl.ds(0, 2 * inner - 1)], GRAM)
        left_here(gb.at[pl.ds(0, outer * n_c - 1)], GRAM + 1)


def flush(*refs):
    sem = refs[-1]
    half = len(refs) // 2
    copies = [
        pltpu.make_async_copy(refs[q], refs[half + q], sem.at[q]) for q in range(half)
    ]
    for copy in copies:
        copy.start()
    for copy in copies:
        copy.wait()


def solution(mesh):
    n_r, n_c = mesh.shape["row"], mesh.shape["col"]
    half = n_r // 2
    inner = 1 << ((half.bit_length() - 1) // 2)
    outer = half // inner

    def per_device(tiles, tile_row, tile_col, right_vecs, left_vecs):
        slots, side = tiles.shape[2], tiles.shape[3]
        piece, vecs, _ = right_vecs.shape
        chunks = 8
        wide = vecs + PAD
        part = piece * wide
        block_rows, block_cols = piece * n_c, piece * n_r
        planes = outer * inner
        near, far, mates = max(inner - 1, 1), max(outer - 1, 1), max(n_c - 1, 1)
        rows = vecs // HALVES
        coded = [((piece * (vecs + 2), side), jnp.int16), ((piece, side), F32)]
        halved = [((piece * (rows + 2), side), jnp.int16), ((piece, side), F32)]
        vmem = pl.BlockSpec(memory_space=pltpu.VMEM)
        dma = pltpu.SemaphoreType.DMA
        shapes = [(piece, vecs, side), (piece, vecs, side), (vecs, vecs)]
        held = pl.pallas_call(
            functools.partial(kernel, (n_r, n_c, outer, inner, chunks)),
            out_shape=tuple(pltpu.VMEM(shape, F32) for shape in shapes),
            in_specs=[pl.BlockSpec(memory_space=pltpu.HBM)] * 5,
            out_specs=(vmem, vmem, vmem),
            scratch_shapes=[
                pltpu.VMEM((slots, side, side), BF16),
                pltpu.VMEM((block_cols, vecs, side), BF16),
                pltpu.VMEM((block_rows, vecs, side), BF16),
                pltpu.VMEM((slots * wide, side), F32),
                pltpu.VMEM((block_cols * wide, side), F32),
                pltpu.VMEM((planes, part, side), F32),
                pltpu.VMEM((piece * vecs, side), F32),
                *[
                    pltpu.VMEM(lead + shape, kind)
                    for lead in [(near, outer)] * 2 + [(far,), (outer,)]
                    for shape, kind in coded
                ],
                pltpu.VMEM((block_rows * wide, side), F32),
                *[pltpu.VMEM((mates, HALVES) + shape, kind) for shape, kind in halved * 2],
                pltpu.VMEM((2 * inner, vecs, vecs), F32),
                pltpu.VMEM((outer * n_c, vecs, vecs), F32),
                *[pltpu.SMEM((1, slots), jnp.int32)] * 2,
                *[pltpu.VMEM((1, slots), jnp.int32)] * 2,
                dma((6,)),
                dma((TILE_COPIES,)),
                dma((GRAM + 2,)),
                dma((n_c,)),
                dma((n_r,)),
                dma((1 + (inner - 1) * outer,)),
                dma((near, outer)),
                dma((outer,)),
                dma((mates, HALVES)),
                dma((2,)),
            ],
            compiler_params=pltpu.CompilerParams(
                collective_id=0, has_side_effects=True, vmem_limit_bytes=44 * 1024 * 1024
            ),
            name="arnoldi_step",
        )(
            *[
                pltpu.with_memory_space_constraint(x, pltpu.HBM)
                for x in (
                    tile_row.reshape(1, slots),
                    tile_col.reshape(1, slots),
                    right_vecs,
                    left_vecs,
                    tiles,
                )
            ]
        )
        held = [pltpu.with_memory_space_constraint(x, pltpu.VMEM) for x in held]
        return pl.pallas_call(
            flush,
            out_shape=tuple(jax.ShapeDtypeStruct(shape, F32) for shape in shapes),
            in_specs=[vmem] * len(shapes),
            out_specs=(pl.BlockSpec(memory_space=pl.ANY),) * len(shapes),
            scratch_shapes=[dma((len(shapes),))],
            name="flush",
        )(*held)

    placed = (
        P("row", "col", None, None, None),
        P("row", "col", None),
        P("row", "col", None),
        P(("row", "col"), None, None),
        P(("row", "col"), None, None),
    )
    return jax.shard_map(
        per_device,
        mesh=mesh,
        in_specs=placed,
        out_specs=(P(("row", "col"), None, None), P(("row", "col"), None, None), P()),
        check_vma=False,
    )
```

time: 30.7 us -> 28.7 us (0.935)
  Pallas kernels: 29.9 us -> 27.9 us
    pallas_call x1, Pallas kernels: 29.2 us -> 27.2 us  [per_device(): pl.pallas_call(functools.partial(kernel, (n_r, n_c, outer, inner, chunks)...]
where the time goes in v3:
time: 28.7 us; the launch traced here: 28.5 us
  Pallas kernels  27.9 us (97%)
  between operations  0.64 us (2%)
    pallas_call x1, Pallas kernels, per_device(): pl.pallas_call(functools.partial(kernel, (n_r, n_c, outer, inner, chunks)...  27.2 us
    pallas_call x1, Pallas kernels, per_device(): pl.pallas_call(flush, out_shape=tuple((jax.ShapeDtypeStruct(shape, F32) f...  0.73 us

profile of v3, /device:TPU:0, one launch (start us, length us, event | category | flops | bytes accessed | tf_op | source)
XLA Modules:
  0.0 28.5 jit_solution(15117241796144471158)
XLA Ops:
  0.6 27.2 %arnoldi_step.1 = (f32[8,32,128]{2,1,0:T(8,128)S(1)}, f32[8,32,128]{2,1,0:T(8,128)S(1)}, f32[32,32]{1,0:T(8,128)S(1)}) custom-call(s32[1,256]{1,0:T(1,128)} %bitcast.2, s32[1,256]{1,0:T(1,128)} %bitcast.3, bf16[8,32,128]{2,1,0:T(8,128)(2,1)} %right.1, bf16[8,32,128]{2,1,0:T(8,128)(2,1)} %left.1, bf16[1,1,256,128,128]{4,3,2,1,0:T(8,128)(2,1)} %tiles.1), custom_call_target="tpu_custom_call" | custom-call | tf_op jit(solution)/shard_map/arnoldi_step/pallas_call | solution.py:521
  27.8 0.7 %flush.1 = (f32[8,32,128]{2,1,0:T(8,128)}, f32[8,32,128]{2,1,0:T(8,128)}, f32[32,32]{1,0:T(8,128)}) custom-call(f32[8,32,128]{2,1,0:T(8,128)S(1)} %get-tuple-element.6.refs_0_, f32[8,32,128]{2,1,0:T(8,128)S(1)} %get-tuple-element.7.refs_1_, f32[32,32]{1,0:T(8,128)S(1)} %get-tuple-element.8.refs_2_), custom_call_target="tpu_custom_call" | custom-call | tf_op jit(solution)/shard_map/flush/pallas_call | solution.py:573

commit v4 on v3

--- a/solution.py
+++ b/solution.py
@@ -80,6 +80,7 @@
     send_sem,
     left_sem,
     right_sem,
+    core_sem,
     zc_sem,
     zx_sem,
     zz_sem,
@@ -188,33 +189,31 @@
     for y in y_far:
         send(left, rv_at(c), left_sem.at[c], (r, y), LEFT)
     for x in xs_of[1:]:
-        send(right, cv_at(r), right_sem.at[r], (row_of(o, x, core), c), RIGHT)
+        send(right, cv_at(r), right_sem.at[r // 2], (row_of(o, x, core), c), RIGHT)
     for z in zs_of[1:]:
-        send(right, cv_at(r), right_sem.at[r], (row_of(z, i, core), c), RIGHT)
-    send(right, cv_at(r), right_sem.at[r], partner, RIGHT)
+        send(right, cv_at(r), right_sem.at[r // 2], (row_of(z, i, core), c), RIGHT)
+    send(right, cv_at(r), core_sem.at[0], partner, RIGHT)
     for ch in range(TILE_COPIES):
         tile_copy(ch).start()
 
     def take_z(d):
         with scope("take_z%d" % d):
             got = row_of(zs_of[d], i, core)
-            landed(cv_at(got), right_sem.at[got])
+            landed(cv_at(got), right_sem.at[got // 2])
             for x in xs_of[1:]:
-                send(cv_at(got), cv_at(got), right_sem.at[got], (row_of(o, x, core), c), RIGHT)
-            send(cv_at(got), cv_at(got), right_sem.at[got], partner, RIGHT)
+                send(cv_at(got), cv_at(got), right_sem.at[got // 2], (row_of(o, x, core), c), RIGHT)
+            send(cv_at(got), cv_at(got), core_sem.at[0], partner, RIGHT)
 
     def take_x(d):
         with scope("take_x%d" % d):
             for x in xs_of[1:]:
                 got = row_of(zs_of[d], x, core)
-                landed(cv_at(got), right_sem.at[got])
-                send(cv_at(got), cv_at(got), right_sem.at[got], partner, RIGHT)
-
-    def take_core(d):
-        with scope("take_c%d" % d):
-            for x in xs_of:
-                got = row_of(zs_of[d], x, 1 - core)
-                landed(cv_at(got), right_sem.at[got])
+                landed(cv_at(got), right_sem.at[got // 2])
+                send(cv_at(got), cv_at(got), core_sem.at[0], partner, RIGHT)
+
+    def take_core():
+        with scope("take_core"):
+            landed(cv.at[pl.ds(0, outer * inner * piece)], core_sem.at[0])
 
     def images(first, last, vec_ref, index, limit, turned):
         for s in range(first * step, last * step, PAIR):
@@ -390,7 +389,7 @@
     todo_x, todo_z = list(z_order), list(z_order)
     paired(todo_x[0])
     give_x(todo_x.pop(0))
-    for d in range(2, outer):
+    for d in range(2, outer - 1):
         take_x(d)
     for d in todo_x:
         paired(d)
@@ -399,17 +398,17 @@
     own_x()
     total = jnp.zeros((2 * vecs, vecs), F32)
     for d in range(outer):
+        if d == outer - 1 > 1:
+            take_x(d)
         total = gram_plane(d, total)
     spread(total[:vecs] + total[vecs:], gb, 1, o * n_c + c, wide_peers)
     while len(todo_x) > 1:
         give_x(todo_x.pop(0))
-    for d in range(outer):
-        take_core(d)
+    take_core()
     first = todo_z.pop(0)
-    pl.when(core == 0)(lambda: give_z(first))
     right_images(0, 2)
+    give_z(first)
     give_x(todo_x.pop(0))
-    pl.when(core == 1)(lambda: give_z(first))
     right_images(2, 5)
     if merging:
         pl.when(middle == 0)(lambda: give_z(2))
@@ -546,7 +545,8 @@
                 dma((TILE_COPIES,)),
                 dma((GRAM + 2,)),
                 dma((n_c,)),
-                dma((n_r,)),
+                dma((outer * inner,)),
+                dma((1,)),
                 dma((1 + (inner - 1) * outer,)),
                 dma((near, outer)),
                 dma((outer,)),

time: 28.7 us -> 28.4 us (0.990)
  Pallas kernels: 27.9 us -> 27.6 us
    pallas_call x1, Pallas kernels: 27.2 us -> 26.9 us  [per_device(): pl.pallas_call(functools.partial(kernel, (n_r, n_c, outer, inner, chunks)...]
where the time goes in v4:
time: 28.4 us; the launch traced here: 28.2 us
  Pallas kernels  27.6 us (97%)
  between operations  0.64 us (2%)
    pallas_call x1, Pallas kernels, per_device(): pl.pallas_call(functools.partial(kernel, (n_r, n_c, outer, inner, chunks)...  26.9 us
    pallas_call x1, Pallas kernels, per_device(): pl.pallas_call(flush, out_shape=tuple((jax.ShapeDtypeStruct(shape, F32) f...  0.73 us

profile of v4, /device:TPU:0, one launch (start us, length us, event | category | flops | bytes accessed | tf_op | source)
XLA Modules:
  0.0 28.2 jit_solution(4817297674813838115)
XLA Ops:
  0.6 26.9 %arnoldi_step.1 = (f32[8,32,128]{2,1,0:T(8,128)S(1)}, f32[8,32,128]{2,1,0:T(8,128)S(1)}, f32[32,32]{1,0:T(8,128)S(1)}) custom-call(s32[1,256]{1,0:T(1,128)} %bitcast.2, s32[1,256]{1,0:T(1,128)} %bitcast.3, bf16[8,32,128]{2,1,0:T(8,128)(2,1)} %right.1, bf16[8,32,128]{2,1,0:T(8,128)(2,1)} %left.1, bf16[1,1,256,128,128]{4,3,2,1,0:T(8,128)(2,1)} %tiles.1), custom_call_target="tpu_custom_call" | custom-call | tf_op jit(solution)/shard_map/arnoldi_step/pallas_call | solution.py:520
  27.5 0.7 %flush.1 = (f32[8,32,128]{2,1,0:T(8,128)}, f32[8,32,128]{2,1,0:T(8,128)}, f32[32,32]{1,0:T(8,128)}) custom-call(f32[8,32,128]{2,1,0:T(8,128)S(1)} %get-tuple-element.6.refs_0_, f32[8,32,128]{2,1,0:T(8,128)S(1)} %get-tuple-element.7.refs_1_, f32[32,32]{1,0:T(8,128)S(1)} %get-tuple-element.8.refs_2_), custom_call_target="tpu_custom_call" | custom-call | tf_op jit(solution)/shard_map/flush/pallas_call | solution.py:573

commit v5 on v4

--- a/solution.py
+++ b/solution.py
@@ -13,7 +13,7 @@
 BF16 = jnp.bfloat16
 PAIR = 2
 HALVES = 2
-TILE_COPIES = 2
+TILE_COPIES = 4
 RIGHT, LEFT, PAIRED, ALONG_X, ALONG_Z, ALONG_Y, GRAM = range(7)
 TOP = 32767.0
 LEAST = 2.0**-110
@@ -50,6 +50,7 @@
     out_z,
     out_g,
     tbuf,
+    tflip,
     cv,
     rv,
     prod,
@@ -129,6 +130,8 @@
     ]
     for copy in own:
         copy.start()
+    for ch in range(TILE_COPIES):
+        tile_copy(ch).start()
 
     barrier = pltpu.get_barrier_semaphore()
     near = [
@@ -193,8 +196,6 @@
     for z in zs_of[1:]:
         send(right, cv_at(r), right_sem.at[r // 2], (row_of(z, i, core), c), RIGHT)
     send(right, cv_at(r), core_sem.at[0], partner, RIGHT)
-    for ch in range(TILE_COPIES):
-        tile_copy(ch).start()
 
     def take_z(d):
         with scope("take_z%d" % d):
@@ -215,17 +216,28 @@
         with scope("take_core"):
             landed(cv.at[pl.ds(0, outer * inner * piece)], core_sem.at[0])
 
-    def images(first, last, vec_ref, index, limit, turned):
+    def turn_tiles():
+        rows = lax.broadcasted_iota(jnp.int32, (side, side), 0)
+        unit = rows == lax.broadcasted_iota(jnp.int32, (side, side), 1)
+        unit = jnp.where(unit, 1.0, 0.0).astype(BF16)
+        for ch in range(TILE_COPIES):
+            with scope("wait_tiles%d" % ch):
+                tile_copy(ch).wait()
+            with scope("turn%d" % ch):
+                part = slots // TILE_COPIES
+                for s in range(ch * part, (ch + 1) * part, PAIR):
+                    for q in range(PAIR):
+                        tflip[s + q] = tbuf[s + q].T
+
+    def images(first, last, tile_ref, vec_ref, index, limit):
         for s in range(first * step, last * step, PAIR):
             xs = [vec_ref[jnp.minimum(index[0, s + q], limit - 1)] for q in range(PAIR)]
-            ts = [tbuf[s + q] for q in range(PAIR)]
-            dims = across if turned else plain
-            got = mul(jnp.concatenate(xs, 0), jnp.concatenate(ts, 0 if turned else 1), dims)
+            ts = [tile_ref[s + q] for q in range(PAIR)]
+            got = mul(jnp.concatenate(xs, 0), jnp.concatenate(ts, 1))
             for q in range(PAIR):
                 block = got[q * vecs : (q + 1) * vecs, q * side : (q + 1) * side]
                 prod[pl.ds((s + q) * wide, vecs), :] = block
 
-    plain = (((1,), (0,)), ((), ()))
     across = (((1,), (1,)), ((), ()))
 
     def gather_sums(index_v, rows, target, first, last):
@@ -355,6 +367,7 @@
                 total = total + buf[q]
             return total
 
+    turn_tiles()
     with scope("wait_left"):
         for copy in own:
             copy.wait()
@@ -363,21 +376,19 @@
 
     def left_images(first, last):
         with scope("imgL%d" % first):
-            images(first, last, rv, row_s, block_rows, False)
+            images(first, last, tbuf, rv, row_s, block_rows)
 
     def right_images(first, last):
         with scope("imgR%d" % first):
-            images(first, last, cv, col_s, block_cols, True)
+            images(first, last, tflip, cv, col_s, block_cols)
 
     def maybe(step, d):
         if d < outer:
             step(d)
 
     maybe(take_z, 1)
-    tile_copy(0).wait()
     left_images(0, chunks // 2)
     take_x(0)
-    tile_copy(1).wait()
     left_images(chunks // 2, chunks)
     maybe(take_z, 2)
     with scope("gatherZ"):
@@ -385,10 +396,10 @@
     for d in range(3, outer):
         take_z(d)
     give_core()
-    maybe(take_x, 1)
     todo_x, todo_z = list(z_order), list(z_order)
     paired(todo_x[0])
     give_x(todo_x.pop(0))
+    maybe(take_x, 1)
     for d in range(2, outer - 1):
         take_x(d)
     for d in todo_x:
@@ -409,13 +420,7 @@
     right_images(0, 2)
     give_z(first)
     give_x(todo_x.pop(0))
-    right_images(2, 5)
-    if merging:
-        pl.when(middle == 0)(lambda: give_z(2))
-        todo_z.remove(2)
-    right_images(5, chunks)
-    while len(todo_z) > 1:
-        give_z(todo_z.pop(0))
+    right_images(2, chunks)
 
     def give_y(h):
         rows = vecs // HALVES
@@ -429,8 +434,13 @@
                 dst = qy.at[d, h], sy.at[d, h]
                 post(out, dst, zy_sem.at[d, h], (r, y), ALONG_Y, rows)
 
+    if merging:
+        pl.when(middle == 0)(lambda: give_z(2))
+        todo_z.remove(2)
     for h in range(HALVES):
         give_y(h)
+    while len(todo_z) > 1:
+        give_z(todo_z.pop(0))
     spread(collect(gb, 1), ga, 0, i * 2 + core, near_peers)
     if merging:
         pl.when(middle == 1)(lambda: give_z(2, [3]))
@@ -523,6 +533,7 @@
             in_specs=[pl.BlockSpec(memory_space=pltpu.HBM)] * 5,
             out_specs=(vmem, vmem, vmem),
             scratch_shapes=[
+                pltpu.VMEM((slots, side, side), BF16),
                 pltpu.VMEM((slots, side, side), BF16),
                 pltpu.VMEM((block_cols, vecs, side), BF16),
                 pltpu.VMEM((block_rows, vecs, side), BF16),

time: 28.4 us -> 28.1 us (0.989)
  Pallas kernels: 27.6 us -> 27.3 us
where the time goes in v5:
time: 28.1 us; the launch traced here: 28 us
  Pallas kernels  27.3 us (97%)
  between operations  0.64 us (2%)
    pallas_call x1, Pallas kernels, per_device(): pl.pallas_call(functools.partial(kernel, (n_r, n_c, outer, inner, chunks)...  26.6 us
    pallas_call x1, Pallas kernels, per_device(): pl.pallas_call(flush, out_shape=tuple((jax.ShapeDtypeStruct(shape, F32) f...  0.73 us

profile of v5, /device:TPU:0, one launch (start us, length us, event | category | flops | bytes accessed | tf_op | source)
XLA Modules:
  0.0 28.0 jit_solution(13621723694805681719)
XLA Ops:
  0.6 26.6 %arnoldi_step.1 = (f32[8,32,128]{2,1,0:T(8,128)S(1)}, f32[8,32,128]{2,1,0:T(8,128)S(1)}, f32[32,32]{1,0:T(8,128)S(1)}) custom-call(s32[1,256]{1,0:T(1,128)} %bitcast.2, s32[1,256]{1,0:T(1,128)} %bitcast.3, bf16[8,32,128]{2,1,0:T(8,128)(2,1)} %right.1, bf16[8,32,128]{2,1,0:T(8,128)(2,1)} %left.1, bf16[1,1,256,128,128]{4,3,2,1,0:T(8,128)(2,1)} %tiles.1), custom_call_target="tpu_custom_call" | custom-call | tf_op jit(solution)/shard_map/arnoldi_step/pallas_call | solution.py:530
  27.2 0.7 %flush.1 = (f32[8,32,128]{2,1,0:T(8,128)}, f32[8,32,128]{2,1,0:T(8,128)}, f32[32,32]{1,0:T(8,128)}) custom-call(f32[8,32,128]{2,1,0:T(8,128)S(1)} %get-tuple-element.6.refs_0_, f32[8,32,128]{2,1,0:T(8,128)S(1)} %get-tuple-element.7.refs_1_, f32[32,32]{1,0:T(8,128)S(1)} %get-tuple-element.8.refs_2_), custom_call_target="tpu_custom_call" | custom-call | tf_op jit(solution)/shard_map/flush/pallas_call | solution.py:584

commit v6 on v5

--- a/solution.py
+++ b/solution.py
@@ -386,10 +386,10 @@
         if d < outer:
             step(d)
 
+    left_images(0, 2)
     maybe(take_z, 1)
-    left_images(0, chunks // 2)
+    left_images(2, chunks)
     take_x(0)
-    left_images(chunks // 2, chunks)
     maybe(take_z, 2)
     with scope("gatherZ"):
         gather_sums(col_v, block_cols, zp, 0, vecs)

time: 28.1 us -> 28.1 us (level)
  no operation moved by 1% of the time
where the time goes in v6:
time: 28.1 us; the launch traced here: 28 us
  Pallas kernels  27.3 us (97%)
  between operations  0.64 us (2%)
    pallas_call x1, Pallas kernels, per_device(): pl.pallas_call(functools.partial(kernel, (n_r, n_c, outer, inner, chunks)...  26.6 us
    pallas_call x1, Pallas kernels, per_device(): pl.pallas_call(flush, out_shape=tuple((jax.ShapeDtypeStruct(shape, F32) f...  0.73 us

profile of v6, /device:TPU:0, one launch (start us, length us, event | category | flops | bytes accessed | tf_op | source)
XLA Modules:
  0.0 28.0 jit_solution(7459281465949320226)
XLA Ops:
  0.6 26.6 %arnoldi_step.1 = (f32[8,32,128]{2,1,0:T(8,128)S(1)}, f32[8,32,128]{2,1,0:T(8,128)S(1)}, f32[32,32]{1,0:T(8,128)S(1)}) custom-call(s32[1,256]{1,0:T(1,128)} %bitcast.2, s32[1,256]{1,0:T(1,128)} %bitcast.3, bf16[8,32,128]{2,1,0:T(8,128)(2,1)} %right.1, bf16[8,32,128]{2,1,0:T(8,128)(2,1)} %left.1, bf16[1,1,256,128,128]{4,3,2,1,0:T(8,128)(2,1)} %tiles.1), custom_call_target="tpu_custom_call" | custom-call | tf_op jit(solution)/shard_map/arnoldi_step/pallas_call | solution.py:530
  27.2 0.7 %flush.1 = (f32[8,32,128]{2,1,0:T(8,128)}, f32[8,32,128]{2,1,0:T(8,128)}, f32[32,32]{1,0:T(8,128)}) custom-call(f32[8,32,128]{2,1,0:T(8,128)S(1)} %get-tuple-element.6.refs_0_, f32[8,32,128]{2,1,0:T(8,128)S(1)} %get-tuple-element.7.refs_1_, f32[32,32]{1,0:T(8,128)S(1)} %get-tuple-element.8.refs_2_), custom_call_target="tpu_custom_call" | custom-call | tf_op jit(solution)/shard_map/flush/pallas_call | solution.py:584

commit v7 on v6

--- a/solution.py
+++ b/solution.py
@@ -390,9 +390,12 @@
     maybe(take_z, 1)
     left_images(2, chunks)
     take_x(0)
-    maybe(take_z, 2)
-    with scope("gatherZ"):
-        gather_sums(col_v, block_cols, zp, 0, vecs)
+    pl.when(core == 1)(lambda: maybe(take_z, 2))
+    with scope("gatherZa"):
+        gather_sums(col_v, block_cols, zp, 0, vecs // 2)
+    pl.when(core == 0)(lambda: maybe(take_z, 2))
+    with scope("gatherZb"):
+        gather_sums(col_v, block_cols, zp, vecs // 2, vecs)
     for d in range(3, outer):
         take_z(d)
     give_core()

time: 28.1 us -> 28.1 us (level)
  no operation moved by 1% of the time
where the time goes in v7:
time: 28.1 us; the launch traced here: 28 us
  Pallas kernels  27.3 us (97%)
  between operations  0.64 us (2%)
    pallas_call x1, Pallas kernels, per_device(): pl.pallas_call(functools.partial(kernel, (n_r, n_c, outer, inner, chunks)...  26.6 us
    pallas_call x1, Pallas kernels, per_device(): pl.pallas_call(flush, out_shape=tuple((jax.ShapeDtypeStruct(shape, F32) f...  0.73 us

profile of v7, /device:TPU:0, one launch (start us, length us, event | category | flops | bytes accessed | tf_op | source)
XLA Modules:
  0.0 28.0 jit_solution(14443165867525551103)
XLA Ops:
  0.6 26.6 %arnoldi_step.1 = (f32[8,32,128]{2,1,0:T(8,128)S(1)}, f32[8,32,128]{2,1,0:T(8,128)S(1)}, f32[32,32]{1,0:T(8,128)S(1)}) custom-call(s32[1,256]{1,0:T(1,128)} %bitcast.2, s32[1,256]{1,0:T(1,128)} %bitcast.3, bf16[8,32,128]{2,1,0:T(8,128)(2,1)} %right.1, bf16[8,32,128]{2,1,0:T(8,128)(2,1)} %left.1, bf16[1,1,256,128,128]{4,3,2,1,0:T(8,128)(2,1)} %tiles.1), custom_call_target="tpu_custom_call" | custom-call | tf_op jit(solution)/shard_map/arnoldi_step/pallas_call | solution.py:533
  27.2 0.7 %flush.1 = (f32[8,32,128]{2,1,0:T(8,128)}, f32[8,32,128]{2,1,0:T(8,128)}, f32[32,32]{1,0:T(8,128)}) custom-call(f32[8,32,128]{2,1,0:T(8,128)S(1)} %get-tuple-element.6.refs_0_, f32[8,32,128]{2,1,0:T(8,128)S(1)} %get-tuple-element.7.refs_1_, f32[32,32]{1,0:T(8,128)S(1)} %get-tuple-element.8.refs_2_), custom_call_target="tpu_custom_call" | custom-call | tf_op jit(solution)/shard_map/flush/pallas_call | solution.py:587
